TPU v7x, 256 devices: a whole 4x4x8 slice. The times are simulated.
256 devices in a mesh: chan: 8 (over y, core), row: 32 (over x, z).
Axes of the slice: x: 4, y: 4, z: 8, core: 2. Of those that a mesh axis runs over, the one named last changes fastest.
Arguments:
- voltages: bfloat16 [256, 2, 8, 1024], P('row', None, 'chan'), may hold values from -6 to 6
- kernels: float32 [256, 2, 4], P('row'), may hold values from 0.1 to 1.9
- footprint: int32 [256, 2], P('row'), may hold values from 0 to 252
- cal_weight: float32 [16, 8], P(None, 'chan'), may hold values from -6 to 6
Outputs:
- power_image: float32 [8, 256, 256], P('chan', None, 'row')
- calibrator_maps: float32 [16, 256, 256], P('chan', None, 'row')
All inputs are finite; a program needn't handle non-finite values.
Results may differ from a plain program's by a relative error of at most 0.004.
Values may be sent and summed in bfloat16 or wider, within the bound.
No kernel may reach another device: no remote copies, remote signals or barrier semaphores. Data moves between devices by JAX's collectives and lax.ppermute only.
A program may use at most 128 MiB of HBM per device.

v0:
```python
import math
import jax
import jax.numpy as jnp
from jax import lax
from jax.sharding import PartitionSpec as P

GRID = 256


def dft_tables(size, first, count):
    indices = jnp.arange(size, dtype=jnp.int32)
    columns = first + jnp.arange(count, dtype=jnp.int32)
    phases = indices[:, None] * columns[None, :] % size
    angles = phases.astype(jnp.float32) * (2.0 * math.pi / size)
    return (jnp.cos(angles), jnp.sin(angles))


def placed(weights, starts, count):
    positions = jnp.arange(count, dtype=jnp.int32)
    taps = jnp.arange(weights.shape[1], dtype=jnp.int32)
    target = starts[:, None] + taps[None, :]
    hit = positions[None, None, :] == target[:, :, None]
    return jnp.sum(jnp.where(hit, weights[:, :, None], jnp.zeros((), weights.dtype)), axis=1)


def blocked_time_sum(values):
    samples = values.shape[-1]
    width = math.gcd(samples, 128)
    shaped = values.reshape(values.shape[:-1] + (samples // width, width))
    return jnp.sum(jnp.sum(shaped, axis=-1), axis=-1)


def image_columns(block):
    highest = lax.Precision.HIGHEST
    cos_table, sin_table = dft_tables(block.shape[1], 0, block.shape[1])
    half_real = block[0]
    half_imag = block[1]
    sky_real = jnp.einsum("umx,ul->lmx", half_real, cos_table, precision=highest) + jnp.einsum(
        "umx,ul->lmx", half_imag, sin_table, precision=highest
    )
    sky_imag = jnp.einsum("umx,ul->lmx", half_imag, cos_table, precision=highest) - jnp.einsum(
        "umx,ul->lmx", half_real, sin_table, precision=highest
    )
    return jnp.stack([sky_real, sky_imag])


def on_device(voltages, kernels, footprint, cal_weight):
    highest = lax.Precision.HIGHEST
    local_stations, _, local_channels, samples = voltages.shape
    row_count = lax.axis_size("row")
    grid_size = GRID
    row_share = grid_size // row_count
    first_row = lax.axis_index("row") * row_share
    columns_total = local_channels * samples
    kernel_taps = kernels.shape[2]
    station_count = local_stations * row_count
    power_scale = 1.0 / (2.0 * samples * station_count * kernel_taps * kernel_taps)
    volt_flat = voltages.reshape(local_stations, 2, columns_total)
    volt_all, kern_all, foot_all = (
        lax.all_gather(volt_flat, "row", axis=0, tiled=True),
        lax.all_gather(kernels.astype(jnp.bfloat16), "row", axis=0, tiled=True).astype(
            kernels.dtype
        ),
        lax.all_gather(footprint, "row", axis=0, tiled=True),
    )
    row_weight = placed(kern_all[:, 0, :], foot_all[:, 0], grid_size)
    col_weight = placed(kern_all[:, 1, :], foot_all[:, 1], grid_size)
    cos_local, sin_local = dft_tables(grid_size, first_row, row_share)
    resp_real = jnp.dot(col_weight, cos_local, precision=highest)
    resp_imag = -jnp.dot(col_weight, sin_local, precision=highest)
    volt_values = volt_all.astype(jnp.float32)
    volt_real = volt_values[:, 0, :]
    volt_imag = volt_values[:, 1, :]
    term_real = (
        resp_real[:, :, None] * volt_real[:, None, :]
        - resp_imag[:, :, None] * volt_imag[:, None, :]
    )
    term_imag = (
        resp_real[:, :, None] * volt_imag[:, None, :]
        + resp_imag[:, :, None] * volt_real[:, None, :]
    )
    terms = jnp.stack([term_real, term_imag], axis=1)
    half_image = jnp.einsum("su,skmx->kumx", row_weight, terms, precision=highest)
    sky = image_columns(half_image)
    squared = sky[0] * sky[0] + sky[1] * sky[1]
    squared = squared.reshape(grid_size, row_share, local_channels, samples)
    power_image = jnp.transpose(blocked_time_sum(squared) * power_scale, (2, 0, 1))
    calibrator_maps = lax.psum_scatter(
        jnp.einsum("qc,clm->qlm", cal_weight, power_image, precision=highest),
        "chan",
        scatter_dimension=0,
        tiled=True,
    )
    return (power_image, calibrator_maps)


def solution(mesh):
    placed = (P("row", None, "chan", None), P("row", None, None), P("row", None), P(None, "chan"))
    return jax.shard_map(
        on_device,
        mesh=mesh,
        in_specs=placed,
        out_specs=(P("chan", None, "row"), P("chan", None, "row")),
        check_vma=False,
    )
```

profile of v0, /device:TPU:2, one launch (start us, length us, event | category | flops | bytes accessed | tf_op | source)
XLA Modules:
  0.0 228.4 jit_solution(15883283409992685155)
XLA Ops:
  7.2 0.0 all-gather.4.cloned.1.call-start
  7.2 0.7 all-gather.4.cloned.1.call-update
  7.9 0.0 reduce-scatter.2.cloned.1.call-start
  7.9 0.7 convert_element_type.22
  8.6 0.1 copy.42
  8.7 45.6 %all-gather.1 = s32[32,8,2]{1,2,0:T(2,128)S(1)} all-gather(s32[1,8,2]{1,2,0:T(2,128)} %bitcast.52), channel_id=1, replica_groups=mesh['chan'=8,'row'=32] {'row'}, dimensions={0}, use_global_device_ids=true | all-gather | bytes 2112 | tf_op jit(solution)/shard_map/all_gather | solution.py:64
  54.3 0.1 reshape.103
  54.4 41.1 %all_gather.10 = bf16[256,2,4]{2,1,0:T(2,128)(2,1)S(1)} all-gather(bf16[8,2,4]{2,1,0:T(2,128)(2,1)S(1)} %copy.42), channel_id=1, replica_groups=mesh['chan'=8,'row'=32] {'row'}, dimensions={0}, use_global_device_ids=true | all-gather | bytes 4224 | tf_op jit(solution)/shard_map/all_gather | solution.py:61
  95.5 0.2 fusion.66
  95.7 0.1 copy.46
  95.8 0.1 copy.43
  95.9 0.3 select_reduce_fusion.1
  96.3 0.3 select_reduce_fusion
  96.6 0.8 convolution_negate_fusion
  97.4 0.9 fusion.26
  98.3 0.0 all-gather.4.cloned.1.call-done
  98.3 2.0 bitcast_convert_fusion
  100.3 1.6 fusion.65
  101.9 1.1 copy.56
  103.0 1.0 copy.57
  104.0 4.2 %multiply_subtract_fusion = (f32[256,1,8,1024]{0,3,2,1:T(8,128)S(1)}, f32[256,1,8,1024]{0,3,2,1:T(8,128)}) fusion(f32[256,1024]{0,1:T(8,128)S(1)} %bitcast.47, f32[256,8]{0,1:T(8,128)S(1)} %convolution_negate_fusion, f32[256,1024]{0,1:T(8,128)S(1)} %bitcast.46, f32[256,8]{0,1:T(8,128)S(1)} %fusion.26), kind=kLoop, calls=%fused_computation.8 | loop fusion | flops 12582912 | bytes 18890752 | tf_op jit(solution)/shard_map/sub | solution.py:75
  108.2 17.8 %fusion.8 = f32[2,256,8,1024]{1,3,2,0:T(8,128)} fusion(f32[256,1,8,1024]{0,3,2,1:T(8,128)} %get-tuple-element.3, f32[256,1,8,1024]{0,3,2,1:T(8,128)S(1)} %get-tuple-element.2, f32[256,256]{1,0:T(8,128)S(1)} %select_reduce_fusion), kind=kOutput, calls=%fused_computation.13 | convolution fusion | flops 12889096192 | bytes 33816576 | tf_op jit(solution)/shard_map/su,skmx->kumx/dot_general | solution.py:83
  126.0 0.0 copy-start
  126.0 13.4 %fusion.6 = f32[256,8,1024]{2,0,1:T(8,128)S(1)} fusion(f32[2,256,8,1024]{1,3,2,0:T(8,128)} %fusion.8), kind=kOutput, calls=%fused_computation.11 | convolution fusion | flops 6443368448 | bytes 16777216 | tf_op jit(solution)/shard_map/umx,ul->lmx/dot_general | solution.py:41
  139.5 0.0 copy-done
  139.5 11.7 %fusion.4 = f32[256,8,1024]{2,0,1:T(8,128)} fusion(f32[2,256,8,1024]{1,3,2,0:T(8,128)S(1)} %copy-done), kind=kOutput, calls=%fused_computation.9 | convolution fusion | flops 6443368448 | bytes 16777216 | tf_op jit(solution)/shard_map/umx,ul->lmx/dot_general | solution.py:41
  151.2 11.4 %fusion.5 = f32[256,8,1024]{2,0,1:T(8,128)} fusion(f32[2,256,8,1024]{1,3,2,0:T(8,128)S(1)} %copy-done), kind=kOutput, calls=%fused_computation.10 | convolution fusion | flops 6443368448 | bytes 16777216 | tf_op jit(solution)/shard_map/umx,ul->lmx/dot_general | solution.py:38
  162.6 0.0 copy-start.1
  162.6 25.1 %add_reduce_fusion = f32[256,8]{0,1:T(8,128)S(1)} fusion(f32[256,8,1024]{2,0,1:T(8,128)S(1)} %fusion.6, f32[256,8,1024]{2,0,1:T(8,128)} %fusion.4, f32[256,8,1024]{2,0,1:T(8,128)} %fusion.5, f32[2,256,8,1024]{1,3,2,0:T(8,128)} %fusion.8), kind=kOutput, calls=%fused_computation.6 | convolution fusion | flops 6455949312 | bytes 33562624 | tf_op jit(solution)/shard_map/umx,ul->lmx/dot_general | solution.py:38
  187.7 0.6 broadcast_multiply_fusion
  188.3 0.0 copy-done.1
  188.3 0.7 multiply_bitcast_fusion
  189.1 0.0 reduce-scatter.2.cloned.1.call-update
  189.1 32.4 %reduce-scatter.2.cloned.1.call-done = f32[2,256,8]{1,2,0:T(8,128)} async-done(((f32[16,256,8]{1,2,0:T(8,128)}), f32[2,256,8]{1,2,0:T(8,128)}) %reduce-scatter.2.cloned.1.call-update) | async-done | bytes 16400 | tf_op jit(solution)/shard_map/reduce_scatter | solution.py:88
  (5 shorter events, 0.0 us)
Async XLA Ops:
  7.2 91.1 %all-gather.4.cloned.1.call-start = ((), (), s32[]{:S(2)}) async-start(), calls=%async_computation.2 | async-start | bytes 1081344 | tf_op jit(solution)/shard_map/all_gather | solution.py:60
  7.9 213.6 %reduce-scatter.2.cloned.1.call-start = ((), (), s32[]{:S(2)}) async-start(), calls=%async_computation.1 | async-start | bytes 147456 | tf_op jit(solution)/shard_map/reduce_scatter | solution.py:88
  126.0 13.5 %copy-start = (f32[2,256,8,1024]{1,3,2,0:T(8,128)S(1)}, f32[2,256,8,1024]{1,3,2,0:T(8,128)}, u32[]{:S(2)}) copy-start(f32[2,256,8,1024]{1,3,2,0:T(8,128)} %fusion.8) | copy-start | bytes 50331652
  162.6 25.7 %copy-start.1 = (f32[16,1]{0,1:T(1,128)S(1)}, f32[16,1]{0,1:T(1,128)}, u32[]{:S(2)}) copy-start(f32[16,1]{0,1:T(1,128)} %param.7) | copy-start | bytes 196
Sparse Core Ops, SparseCore 0:
  10.6 78.1 all-gather.3
  189.2 32.2 reduce-scatter.1
where the time goes:
time: 229 us; the launch traced here: 228 us
  blocking collectives  86.7 us (38%)
  matrix products  81.1 us (35%)
  waiting for transfers between devices  33.1 us (14%)
  between operations  14.1 us (6%)
  other arithmetic  8.93 us (4%)
  local copies, waits for them, and re-layouts  4.26 us (2%)
    all_gather x1, blocking collectives, on_device(): lax.all_gather(footprint, 'row', axis=0, tiled=True)  45.6 us
    all_gather x1, blocking collectives, on_device(): lax.all_gather(kernels.astype(jnp.bfloat16), 'row', axis=0, tiled=True)  41.1 us
    reduce_scatter x1, waiting for transfers between devices, on_device(): lax.psum_scatter(jnp.einsum('qc,clm->qlm', cal_weight, power_image, preci...  32.4 us
    dot_general x1, matrix products, image_columns(): jnp.einsum('umx,ul->lmx', half_imag, sin_table, precision=highest)  25.1 us
    dot_general x1, matrix products, on_device(): jnp.einsum('su,skmx->kumx', row_weight, terms, precision=highest)  17.8 us
    dot_general x1, matrix products, image_columns(): jnp.einsum('umx,ul->lmx', half_imag, cos_table, precision=highest)  13.4 us
    dot_general x1, matrix products, image_columns(): jnp.einsum('umx,ul->lmx', half_real, sin_table, precision=highest)  11.7 us
    dot_general x1, matrix products, image_columns(): jnp.einsum('umx,ul->lmx', half_real, cos_table, precision=highest)  11.4 us
  transfers between devices with their start and end apart: 2, of which 1 were waited for; matrix products, arithmetic and copies ran while one was open for 2% of the time, Pallas kernels for 0%

commit v1 on v0

--- a/solution.py
+++ b/solution.py
@@ -5,6 +5,11 @@
 from jax.sharding import PartitionSpec as P
 
 GRID = 256
+
+
+def all_by_exchange(array, axis, dim):
+    sent = jnp.stack([array] * lax.axis_size(axis))
+    return jnp.concatenate(lax.all_to_all(sent, axis, 0, 0), axis=dim)
 
 
 def dft_tables(size, first, count):
@@ -61,7 +66,7 @@
         lax.all_gather(kernels.astype(jnp.bfloat16), "row", axis=0, tiled=True).astype(
             kernels.dtype
         ),
-        lax.all_gather(footprint, "row", axis=0, tiled=True),
+        all_by_exchange(footprint, "row", 0),
     )
     row_weight = placed(kern_all[:, 0, :], foot_all[:, 0], grid_size)
     col_weight = placed(kern_all[:, 1, :], foot_all[:, 1], grid_size)

time: 229 us -> 219 us (0.956)
  blocking collectives: 86.7 us -> 42.8 us
  waiting for transfers between devices: 33.1 us -> 54.3 us
  starting transfers between devices: 0.08 us -> 11.7 us
    all_gather x1 -> x0, blocking collectives: 45.6 us -> none  [on_device(): lax.all_gather(footprint, 'row', axis=0, tiled=True)]
    all_gather x1, waiting for transfers between devices: 0.01 us -> 21.5 us  [on_device(): lax.all_gather(volt_flat, 'row', axis=0, tiled=True)]
    all_to_all x0 -> x1, starting transfers between devices: none -> 11.6 us  [all_by_exchange(): return jnp.concatenate(lax.all_to_all(sent, axis, 0, 0), axis=dim)]
  transfers between devices with their start and end apart: 2 -> 3, of which waited for: 1 -> 2; matrix products, arithmetic and copies ran while one was open for 2% -> 2% of each run, Pallas kernels for 0% -> 0%
where the time goes in v1:
time: 219 us; the launch traced here: 218 us
  matrix products  81.2 us (37%)
  waiting for transfers between devices  54.3 us (25%)
  blocking collectives  42.8 us (20%)
  between operations  14.1 us (6%)
  starting transfers between devices  11.7 us (5%)
  other arithmetic  8.88 us (4%)
  local copies, waits for them, and re-layouts  5.57 us (3%)
    all_gather x1, blocking collectives, on_device(): lax.all_gather(kernels.astype(jnp.bfloat16), 'row', axis=0, tiled=True)  42.8 us
    reduce_scatter x1, waiting for transfers between devices, on_device(): lax.psum_scatter(jnp.einsum('qc,clm->qlm', cal_weight, power_image, preci...  32.1 us
    dot_general x1, matrix products, image_columns(): jnp.einsum('umx,ul->lmx', half_imag, sin_table, precision=highest)  25.1 us
    all_gather x1, waiting for transfers between devices, on_device(): lax.all_gather(volt_flat, 'row', axis=0, tiled=True)  21.5 us
    dot_general x1, matrix products, on_device(): jnp.einsum('su,skmx->kumx', row_weight, terms, precision=highest)  17.8 us
    dot_general x1, matrix products, image_columns(): jnp.einsum('umx,ul->lmx', half_imag, cos_table, precision=highest)  13.4 us
    dot_general x1, matrix products, image_columns(): jnp.einsum('umx,ul->lmx', half_real, sin_table, precision=highest)  11.8 us
    all_to_all x1, starting transfers between devices, all_by_exchange(): return jnp.concatenate(lax.all_to_all(sent, axis, 0, 0), axis=dim)  11.6 us
  transfers between devices with their start and end apart: 3, of which 2 were waited for; matrix products, arithmetic and copies ran while one was open for 2% of the time, Pallas kernels for 0%

profile of v1, /device:TPU:2, one launch (start us, length us, event | category | flops | bytes accessed | tf_op | source)
XLA Modules:
  0.0 218.5 jit_solution(8874965925855977712)
XLA Ops:
  7.2 0.0 all-gather.3.cloned.1.call-start
  7.2 0.7 all-gather.3.cloned.1.call-update
  7.9 1.3 stack.4
  9.2 11.6 %all-to-all-start = ((s32[32,8,2]{1,2,0:T(2,128)}), s32[32,8,2]{1,2,0:T(2,128)S(1)}, u32[]{:S(2)}, u32[]{:S(2)}) async-start(s32[32,8,2]{1,2,0:T(2,128)} %stack.4), calls=%async_computation | async-start | bytes 65536 | tf_op jit(solution)/shard_map/all_to_all | solution.py:12
  20.8 0.0 reduce-scatter.2.cloned.1.call-start
  20.9 0.7 convert_element_type.22
  21.6 0.1 copy.50
  21.7 42.8 %all_gather.6 = bf16[256,2,4]{2,1,0:T(2,128)(2,1)S(1)} all-gather(bf16[8,2,4]{2,1,0:T(2,128)(2,1)S(1)} %copy.50), channel_id=1, replica_groups=mesh['chan'=8,'row'=32] {'row'}, dimensions={0}, use_global_device_ids=true | all-gather | bytes 4224 | tf_op jit(solution)/shard_map/all_gather | solution.py:66
  64.4 0.2 fusion.66
  64.6 0.1 copy.54
  64.7 0.1 copy.51
  64.8 0.0 all-to-all-done
  64.8 0.1 reshape.103
  64.9 0.3 select_reduce_fusion.1
  65.3 0.3 select_reduce_fusion
  65.6 0.8 convolution_negate_fusion
  66.4 0.9 fusion.26
  67.3 21.5 %all-gather.3.cloned.1.call-done = bf16[256,2,1,1024]{3,1,2,0:T(2,128)(2,1)} async-done(((bf16[8,2,1,1024]{3,1,2,0:T(2,128)(2,1)}), bf16[256,2,1,1024]{3,1,2,0:T(2,128)(2,1)}) %all-gather.3.cloned.1.call-update) | async-done | bytes 1048592 | tf_op jit(solution)/shard_map/all_gather | solution.py:65
  88.7 1.9 bitcast_convert_fusion
  90.7 1.6 fusion.65
  92.3 1.1 copy.64
  93.5 1.0 copy.65
  94.4 4.2 %multiply_subtract_fusion = (f32[256,1,8,1024]{0,3,2,1:T(8,128)S(1)}, f32[256,1,8,1024]{0,3,2,1:T(8,128)}) fusion(f32[256,1024]{0,1:T(8,128)S(1)} %bitcast.46, f32[256,8]{0,1:T(8,128)S(1)} %convolution_negate_fusion, f32[256,1024]{0,1:T(8,128)S(1)} %bitcast.45, f32[256,8]{0,1:T(8,128)S(1)} %fusion.26), kind=kLoop, calls=%fused_computation.8 | loop fusion | flops 12582912 | bytes 18890752 | tf_op jit(solution)/shard_map/sub | solution.py:80
  98.6 17.8 %fusion.8 = f32[2,256,8,1024]{1,3,2,0:T(8,128)} fusion(f32[256,1,8,1024]{0,3,2,1:T(8,128)} %get-tuple-element.3, f32[256,1,8,1024]{0,3,2,1:T(8,128)S(1)} %get-tuple-element.2, f32[256,256]{1,0:T(8,128)S(1)} %select_reduce_fusion), kind=kOutput, calls=%fused_computation.13 | convolution fusion | flops 12889096192 | bytes 33816576 | tf_op jit(solution)/shard_map/su,skmx->kumx/dot_general | solution.py:88
  116.5 0.0 copy-start
  116.5 13.4 %fusion.6 = f32[256,8,1024]{2,0,1:T(8,128)S(1)} fusion(f32[2,256,8,1024]{1,3,2,0:T(8,128)} %fusion.8), kind=kOutput, calls=%fused_computation.11 | convolution fusion | flops 6443368448 | bytes 16777216 | tf_op jit(solution)/shard_map/umx,ul->lmx/dot_general | solution.py:46
  129.9 0.0 copy-done
  129.9 11.8 %fusion.4 = f32[256,8,1024]{2,0,1:T(8,128)} fusion(f32[2,256,8,1024]{1,3,2,0:T(8,128)S(1)} %copy-done), kind=kOutput, calls=%fused_computation.9 | convolution fusion | flops 6443368448 | bytes 16777216 | tf_op jit(solution)/shard_map/umx,ul->lmx/dot_general | solution.py:46
  141.7 11.4 %fusion.5 = f32[256,8,1024]{2,0,1:T(8,128)} fusion(f32[2,256,8,1024]{1,3,2,0:T(8,128)S(1)} %copy-done), kind=kOutput, calls=%fused_computation.10 | convolution fusion | flops 6443368448 | bytes 16777216 | tf_op jit(solution)/shard_map/umx,ul->lmx/dot_general | solution.py:43
  153.1 0.0 copy-start.1
  153.1 25.1 %add_reduce_fusion = f32[256,8]{0,1:T(8,128)S(1)} fusion(f32[256,8,1024]{2,0,1:T(8,128)S(1)} %fusion.6, f32[256,8,1024]{2,0,1:T(8,128)} %fusion.4, f32[256,8,1024]{2,0,1:T(8,128)} %fusion.5, f32[2,256,8,1024]{1,3,2,0:T(8,128)} %fusion.8), kind=kOutput, calls=%fused_computation.6 | convolution fusion | flops 6455949312 | bytes 33562624 | tf_op jit(solution)/shard_map/umx,ul->lmx/dot_general | solution.py:43
  178.2 0.6 broadcast_multiply_fusion
  178.8 0.0 copy-done.1
  178.8 0.7 multiply_bitcast_fusion
  179.5 0.0 reduce-scatter.2.cloned.1.call-update
  179.6 32.1 %reduce-scatter.2.cloned.1.call-done = f32[2,256,8]{1,2,0:T(8,128)} async-done(((f32[16,256,8]{1,2,0:T(8,128)}), f32[2,256,8]{1,2,0:T(8,128)}) %reduce-scatter.2.cloned.1.call-update) | async-done | bytes 16400 | tf_op jit(solution)/shard_map/reduce_scatter | solution.py:93
  (5 shorter events, 0.0 us)
Async XLA Ops:
  7.2 81.6 %all-gather.3.cloned.1.call-start = ((), (), s32[]{:S(2)}) async-start(), calls=%async_computation.3 | async-start | bytes 1081344 | tf_op jit(solution)/shard_map/all_gather | solution.py:65
  9.2 55.6 %all-to-all-start = ((s32[32,8,2]{1,2,0:T(2,128)}), s32[32,8,2]{1,2,0:T(2,128)S(1)}, u32[]{:S(2)}, u32[]{:S(2)}) async-start(s32[32,8,2]{1,2,0:T(2,128)} %stack.4), calls=%async_computation | async-start | bytes 65536 | tf_op jit(solution)/shard_map/all_to_all | solution.py:12
  20.8 190.8 %reduce-scatter.2.cloned.1.call-start = ((), (), s32[]{:S(2)}) async-start(), calls=%async_computation.2 | async-start | bytes 147456 | tf_op jit(solution)/shard_map/reduce_scatter | solution.py:93
  116.5 13.5 %copy-start = (f32[2,256,8,1024]{1,3,2,0:T(8,128)S(1)}, f32[2,256,8,1024]{1,3,2,0:T(8,128)}, u32[]{:S(2)}) copy-start(f32[2,256,8,1024]{1,3,2,0:T(8,128)} %fusion.8) | copy-start | bytes 50331652
  153.1 25.7 %copy-start.1 = (f32[16,1]{0,1:T(1,128)S(1)}, f32[16,1]{0,1:T(1,128)}, u32[]{:S(2)}) copy-start(f32[16,1]{0,1:T(1,128)} %param.7) | copy-start | bytes 196
Sparse Core Ops, SparseCore 0:
  10.6 78.1 all-gather.2
  179.7 31.9 reduce-scatter.1
